TPU v7x, 256 devices: a whole 4x4x8 slice. The times are simulated.
256 devices in a mesh: seq: 16 (over z, x_lo), wr: 4 (over y), wc: 4 (over x_hi, core).
Axes of the slice: x: 4 (x_hi: 2, x_lo: 2; x = x_hi * 2 + x_lo), y: 4, z: 8, core: 2. Of those that a mesh axis runs over, the one named last changes fastest.
Arguments:
- tokens: bfloat16 [8192, 2048], P('seq', ('wr', 'wc')), may hold values from -6 to 6
- ln_gain: float32 [2, 2048], replicated, may hold values from 0.5 to 1.5
- w_branch: bfloat16 [2, 2048, 4096], P(None, None, ('wr', 'wc')), may hold values from -0.125 to 0.125
- w_outgate: bfloat16 [2, 2048, 4096], P(None, None, ('wr', 'wc')), may hold values from -0.125 to 0.125
- w_gates: bfloat16 [2, 2048, 8], replicated, may hold values from -0.125 to 0.125
- forget_bias: float32 [2, 4], replicated, may hold values from 3.2 to 11
- conv_weight: float32 [2, 4, 4096], P(None, None, ('wr', 'wc')), may hold values from -3 to 3
- conv_bias: float32 [2, 4096], P(None, ('wr', 'wc')), may hold values from -3 to 3
- w_query: float32 [2, 4, 4, 4, 256], P(None, 'wr'), may hold values from -3 to 3
- w_key: float32 [2, 4, 4, 4, 256], P(None, 'wr'), may hold values from -3 to 3
- w_value: float32 [2, 4, 4, 4, 256], P(None, 'wr', None, 'wc'), may hold values from -4 to 4
- skip_gain: float32 [2, 4096], P(None, ('wr', 'wc')), may hold values from 0.5 to 1.5
- norm_gain: float32 [2, 4096], P(None, ('wr', 'wc')), may hold values from 0.5 to 1.5
- w_down: bfloat16 [2, 4096, 2048], P(None, ('wr', 'wc')), may hold values from -0.125 to 0.125
- lengths: int32 [3], replicated, may hold values from 1 to 4096, 8192 in all
- request_prompt: int32 [32], P('seq'), may hold values from 0 to 2
Outputs:
- mixed: bfloat16 [8192, 2048], P('seq', ('wr', 'wc'))
- request_state: bfloat16 [2, 32, 4, 1024, 1024], P(None, 'seq', 'wr', None, 'wc')
- request_conv: bfloat16 [2, 32, 3, 4096], P(None, 'seq', None, ('wr', 'wc'))
Inputs may be any that keep to these rules, and one draw needn't show every extreme that they name: `lengths`: the 3 prompts lie end to end in order and fill all 8192 positions; the longest has exactly 4096 positions.
All inputs are finite; a program needn't handle non-finite values.
Results may differ from a plain program's by a relative error of at most 0.035.
Values may be sent and summed in bfloat16 or wider, within the bound.
A program may use at most 128 MiB of HBM per device.

v0:
```python
import jax
import jax.numpy as jnp
from jax import lax
from jax.sharding import PartitionSpec as P

HEADS = 4
CONV = 4
LAYERS = 2
PROMPTS = 3
EPSILON = 1e-05
GATE_CAP = 15.0
ROW_DIMS = (((0,), (0,)), ((), ()))
FEATURE_DIMS = (((1,), (1,)), ((), ()))


def shifted(value, axis, steps):
    count = lax.axis_size(axis)
    first, last = (max(0, -steps), min(count, count - steps))
    return lax.ppermute(value, axis, [(source, source + steps) for source in range(first, last)])


def span_weights(gathered, lengths, rows, count):
    spans = jnp.arange(count, dtype=jnp.int32)
    seg_end = segment_of(spans * rows + (rows - 1), lengths)
    totals = gathered[:, 0]
    later = jnp.arange(count + 1, dtype=jnp.int32)
    between = (spans[None, None, :] > spans[None, :, None]) & (
        spans[None, None, :] < later[:, None, None]
    )
    logs = jnp.sum(jnp.where(between, totals[None, None, :], 0.0), axis=2)
    seg_in = segment_of(later * rows - 1, lengths)
    keep = (spans[None, :] < later[:, None]) & (seg_end[None, :] == seg_in[:, None])
    state_rows = jnp.where(keep, jnp.exp(logs), 0.0)
    end_rows = []
    for prompt, end_pos in enumerate((lengths[0] - 1, lengths[0] + lengths[1] - 1)):
        holder = end_pos // rows
        pick = (spans == holder).astype(jnp.float32)
        end_cum = jnp.sum(pick * gathered[:, 1 + prompt])
        row = jnp.sum(pick[:, None] * logs[:count], axis=0) + end_cum
        kept = (spans < holder) & (seg_end == prompt)
        kept = kept & (segment_of(holder * rows - 1, lengths) == prompt)
        end_rows.append(jnp.where(kept, jnp.exp(row), 0.0))
    return (state_rows[:count], jnp.stack(end_rows + [state_rows[count]]))


def mix_spans(weights, spans):
    return jnp.sum(weights[:, :, None, None] * spans[None], axis=1)


def norm_rows(source, gain_row):
    widened = source.astype(jnp.float32)
    row_mean = jnp.mean(widened, axis=1, keepdims=True)
    row_var = jnp.mean(widened * widened, axis=1, keepdims=True) - row_mean * row_mean
    return ((widened - row_mean) * lax.rsqrt(row_var + EPSILON) * gain_row).astype(jnp.bfloat16)


def segment_of(positions, lengths):
    bound_one = lengths[0]
    bound_two = lengths[0] + lengths[1]
    return (positions >= bound_one).astype(jnp.int32) + (positions >= bound_two).astype(jnp.int32)


def conv_rows(extended, ext_segment, segment, weight, bias_row):
    row_count = segment.shape[0]
    widened = extended.astype(jnp.float32)
    summed = jnp.zeros((row_count, widened.shape[1]), jnp.float32) + bias_row
    for back_step in range(weight.shape[0]):
        low_row = weight.shape[0] - 1 - back_step
        keep_row = (ext_segment[low_row : low_row + row_count] == segment).astype(jnp.float32)
        summed = (
            summed + weight[back_step] * widened[low_row : low_row + row_count] * keep_row[:, None]
        )
    return jax.nn.silu(summed).astype(jnp.bfloat16)


def block_mix(source, weight):
    row_count = source.shape[0]
    grouped = source.astype(jnp.float32).reshape(row_count, 4, -1)
    mixed = jnp.einsum("tig,ijg->tjg", grouped, weight, precision=lax.Precision.HIGHEST)
    return mixed.reshape(row_count, -1)


def block_terms(queries, key_rows, values, log_forget, in_gate, segment, prev_seg):
    row_count = queries.shape[0]
    cum_log = jnp.cumsum(log_forget)
    row_order = jnp.arange(row_count)
    allowed = (row_order[:, None] >= row_order[None, :]) & (segment[:, None] == segment[None, :])
    exponent = jnp.where(allowed, cum_log[:, None] - cum_log[None, :] + in_gate[None, :], -jnp.inf)
    scores = lax.dot_general(
        queries, key_rows, FEATURE_DIMS, preferred_element_type=jnp.float32
    ) * jnp.exp(exponent)
    in_block = jnp.dot(scores.astype(jnp.bfloat16), values, preferred_element_type=jnp.float32)
    carried = jnp.where(segment == prev_seg, jnp.exp(cum_log), 0.0)
    last_seg = segment[row_count - 1]
    weights = jnp.where(
        segment == last_seg, jnp.exp(cum_log[row_count - 1] - cum_log + in_gate), 0.0
    )
    weighted = (key_rows.astype(jnp.float32) * weights[:, None]).astype(jnp.bfloat16)
    increment = lax.dot_general(weighted, values, ROW_DIMS, preferred_element_type=jnp.float32)
    return (in_block, carried, increment)


def end_part(key_rows, values, cum_log, in_gate, segment, local_end, prompt, holder):
    row_order = jnp.arange(segment.shape[0])
    chosen = holder & (segment == prompt) & (row_order <= local_end)
    weights = jnp.where(chosen, jnp.exp(cum_log[local_end] - cum_log + in_gate), 0.0)
    weighted = (key_rows.astype(jnp.float32) * weights[:, None]).astype(jnp.bfloat16)
    return lax.dot_general(weighted, values, ROW_DIMS, preferred_element_type=jnp.float32)


def body(
    tokens,
    ln_gain,
    w_branch,
    w_outgate,
    w_gates,
    forget_bias,
    conv_weight,
    conv_bias,
    w_query,
    w_key,
    w_value,
    skip_gain,
    norm_gain,
    w_down,
    lengths,
    request_prompt,
):
    tok_rows = tokens.shape[0]
    seq_count = lax.axis_size("seq")
    seq_index = lax.axis_index("seq")
    head_idx = lax.axis_index("wr")
    row_offset = seq_index * tok_rows
    total_rows = tok_rows * seq_count
    row_ids = jnp.arange(tok_rows, dtype=jnp.int32)
    positions = row_offset + row_ids
    segment = segment_of(positions, lengths)
    seg_before = jnp.where(row_offset > 0, segment_of(row_offset - 1, lengths), -1)
    rim_positions = row_offset - (CONV - 1) + jnp.arange(CONV - 1, dtype=jnp.int32)
    rim_segment = jnp.where(rim_positions >= 0, segment_of(rim_positions, lengths), -1)
    ext_segment = jnp.concatenate([rim_segment, segment])
    prompt_starts = [jnp.zeros((), jnp.int32), lengths[0], lengths[0] + lengths[1]]
    prompt_ends = [
        lengths[0] - 1,
        lengths[0] + lengths[1] - 1,
        jnp.zeros((), jnp.int32) + (total_rows - 1),
    ]
    head_mask = (jnp.arange(HEADS, dtype=jnp.int32) == head_idx).astype(jnp.float32)
    current = tokens
    sent_states = []
    sent_edges = []
    for layer_idx in range(LAYERS):
        gathered = lax.all_gather(current, ("wr", "wc"), axis=1, tiled=True)
        normed = norm_rows(gathered, ln_gain[layer_idx])
        branch = jnp.dot(normed, w_branch[layer_idx], preferred_element_type=jnp.float32).astype(
            jnp.bfloat16
        )
        outgate = jnp.dot(normed, w_outgate[layer_idx], preferred_element_type=jnp.float32)
        gate_pre = jnp.dot(normed, w_gates[layer_idx], preferred_element_type=jnp.float32)
        input_pre = jnp.sum(gate_pre[:, :HEADS] * head_mask, axis=1)
        forget_pre = jnp.sum((gate_pre[:, HEADS:] + forget_bias[layer_idx]) * head_mask, axis=1)
        in_gate = GATE_CAP * jnp.tanh(input_pre / GATE_CAP)
        log_forget = jax.nn.log_sigmoid(forget_pre)
        edge_in = shifted(branch[tok_rows - (CONV - 1) :], "seq", 1)
        extended = jnp.concatenate([edge_in, branch], axis=0)
        conv_act = conv_rows(
            extended, ext_segment, segment, conv_weight[layer_idx], conv_bias[layer_idx]
        )
        head_branch, head_act = (
            lax.all_gather(branch, "wc", axis=1, tiled=True),
            lax.all_gather(conv_act, "wc", axis=1, tiled=True),
        )
        head_width = head_act.shape[1]
        queries = block_mix(head_act, w_query[layer_idx, 0]).astype(jnp.bfloat16)
        key_rows = (block_mix(head_act, w_key[layer_idx, 0]) * head_width ** (-0.5)).astype(
            jnp.bfloat16
        )
        values = block_mix(head_branch, w_value[layer_idx, 0]).astype(jnp.bfloat16)
        cum_log = jnp.cumsum(log_forget)
        holders = [
            (end_pos >= row_offset) & (end_pos < row_offset + tok_rows) for end_pos in prompt_ends
        ]
        local_ends = [jnp.clip(end_pos - row_offset, 0, tok_rows - 1) for end_pos in prompt_ends]
        span_logs = lax.all_gather(
            jnp.stack([cum_log[tok_rows - 1], cum_log[local_ends[0]], cum_log[local_ends[1]]]),
            "seq",
        )
        state_rows, end_rows = span_weights(span_logs, lengths, tok_rows, seq_count)
        in_block, carried, increment = block_terms(
            queries, key_rows, values, log_forget, in_gate, segment, seg_before
        )
        parts = [increment] + [
            end_part(
                key_rows,
                values,
                cum_log,
                in_gate,
                segment,
                local_ends[prompt],
                prompt,
                holders[prompt],
            )
            for prompt in range(PROMPTS - 1)
        ]
        slab = head_width // seq_count
        sent = jnp.stack(
            [part.astype(jnp.bfloat16).reshape(seq_count, slab, -1) for part in parts], axis=1
        )
        got = lax.all_to_all(sent, "seq", 0, 0, tiled=True).astype(jnp.float32)
        spans = got[:, 0]
        states = mix_spans(state_rows, spans).astype(jnp.bfloat16)
        state_here = lax.all_to_all(states, "seq", 0, 0, tiled=True).reshape(head_width, -1)
        own_ends = jnp.sum(got[:, 1:], axis=0)
        ends = mix_spans(end_rows, spans) + jnp.concatenate(
            [own_ends, jnp.zeros_like(own_ends[:1])], axis=0
        )
        sent_states.append(lax.all_gather(ends.astype(jnp.bfloat16), "seq", axis=1, tiled=True))
        hidden_parts = in_block + carried[:, None] * jnp.dot(
            queries, state_here, preferred_element_type=jnp.float32
        )
        sums_one, sums_two = lax.psum(
            (jnp.sum(hidden_parts, axis=1), jnp.sum(hidden_parts * hidden_parts, axis=1)), "wc"
        )
        row_mean = sums_one / head_width
        row_var = sums_two / head_width - row_mean * row_mean
        normal_rows = (hidden_parts - row_mean[:, None]) * lax.rsqrt(row_var + EPSILON)[:, None]
        gated = (
            (
                normal_rows * norm_gain[layer_idx]
                + skip_gain[layer_idx] * conv_act.astype(jnp.float32)
            )
            * jax.nn.silu(outgate)
        ).astype(jnp.bfloat16)
        term_rows = jnp.dot(gated, w_down[layer_idx], preferred_element_type=jnp.float32)
        terms = lax.all_to_all(
            term_rows.astype(jnp.bfloat16), ("wr", "wc"), 1, 0, tiled=True
        ).reshape(-1, tok_rows, current.shape[1])
        summed = jnp.sum(terms.astype(jnp.float32), axis=0)
        current = (current.astype(jnp.float32) + summed).astype(jnp.bfloat16)
        for prompt in range(PROMPTS):
            window = lax.dynamic_slice_in_dim(extended, local_ends[prompt] + 1, CONV - 1, 0)
            edge_pos = prompt_ends[prompt] - (CONV - 2) + jnp.arange(CONV - 1, dtype=jnp.int32)
            sent_edges.append(
                jnp.where(
                    ((edge_pos >= prompt_starts[prompt]) & holders[prompt])[:, None],
                    window,
                    jnp.zeros_like(window),
                )
            )
    state_stack = jnp.stack(sent_states)
    edge_stack = lax.psum(jnp.stack(sent_edges), "seq")
    edge_stack = edge_stack.reshape(LAYERS, PROMPTS, edge_stack.shape[1], edge_stack.shape[2])
    chooser = (request_prompt[:, None] == jnp.arange(PROMPTS, dtype=jnp.int32)[None, :]).astype(
        jnp.bfloat16
    )
    request_state = jnp.einsum(
        "rp,lphd->lrhd", chooser, state_stack, preferred_element_type=jnp.float32
    ).astype(jnp.bfloat16)[:, :, None]
    request_conv = jnp.einsum(
        "rp,lpkc->lrkc", chooser, edge_stack, preferred_element_type=jnp.float32
    ).astype(jnp.bfloat16)
    return (current, request_state, request_conv)


def solution(mesh):
    return jax.shard_map(
        body,
        mesh=mesh,
        in_specs=(
            P("seq", ("wr", "wc")),
            P(),
            P(None, None, ("wr", "wc")),
            P(None, None, ("wr", "wc")),
            P(),
            P(),
            P(None, None, ("wr", "wc")),
            P(None, ("wr", "wc")),
            P(None, "wr", None, None, None),
            P(None, "wr", None, None, None),
            P(None, "wr", None, "wc", None),
            P(None, ("wr", "wc")),
            P(None, ("wr", "wc")),
            P(None, ("wr", "wc"), None),
            P(),
            P("seq"),
        ),
        out_specs=(
            P("seq", ("wr", "wc")),
            P(None, "seq", "wr", None, "wc"),
            P(None, "seq", None, ("wr", "wc")),
        ),
        check_vma=False,
    )
```

profile of v0, /device:TPU:16, one launch (start us, length us, event | category | flops | bytes accessed | tf_op | source)
XLA Modules:
  0.0 664.2 jit_solution(5510766327636577990)
XLA Ops:
  14.5 49.2 %all-gather.11.cloned.1.call-done = bf16[512,2048]{1,0:T(8,128)(2,1)} async-done(((bf16[512,128]{1,0:T(8,128)(2,1)}), bf16[512,2048]{1,0:T(8,128)(2,1)}) %all-gather.11.cloned.1.call-update) | async-done | bytes 2097168 | tf_op jit(solution)/shard_map/all_gather | solution.py:153
  83.3 3.7 exponential_select_fusion.7
  86.9 5.6 all-gather.15.cloned.1.call-done
  96.0 21.3 %all-gather.13.cloned.1.call-done = bf16[512,1024]{1,0:T(8,128)(2,1)} async-done(((bf16[512,256]{1,0:T(8,128)(2,1)}), bf16[512,1024]{1,0:T(8,128)(2,1)}) %all-gather.13.cloned.1.call-update) | async-done | bytes 1048592 | tf_op jit(solution)/shard_map/all_gather | solution.py:171
  136.0 7.3 %all-to-all-start = ((bf16[16,3,64,256]{3,2,1,0:T(8,128)(2,1)}), bf16[16,3,64,256]{3,2,1,0:T(8,128)(2,1)}, u32[]{:S(2)}, u32[]{:S(2)}) async-start(bf16[16,3,64,256]{3,2,1,0:T(8,128)(2,1)} %pad_maximum_fusion.6), calls=%async_computation | async-start | bytes 3145728 | tf_op jit(solution)/shard_map/all_to_all | solution.py:209
  149.7 56.5 %all-reduce.2 = f32[48]{0:T(128)S(1)} all-reduce(f32[48]{0:T(128)S(1)} %maximum_dynamic-update-slice_fusion), channel_id=2, replica_groups=mesh['seq'=16,'wr'=4,'wc'=4] {'seq'}, use_global_device_ids=true, to_apply=%add.2 | all-reduce | flops 48 | bytes 384
  213.4 6.7 %all-to-all-start.1 = ((bf16[16,64,256]{2,1,0:T(8,128)(2,1)}), bf16[16,64,256]{2,1,0:T(8,128)(2,1)}, u32[]{:S(2)}, u32[]{:S(2)}) async-start(bf16[16,64,256]{2,1,0:T(8,128)(2,1)} %multiply_reduce_fusion.1), calls=%async_computation.1 | async-start | bytes 1048576 | tf_op jit(solution)/shard_map/all_to_all | solution.py:212
  236.5 7.1 %all-reduce.5 = (f32[512]{0:T(512)S(1)}, f32[512]{0:T(512)S(1)}) all-reduce(f32[512]{0:T(512)S(1)} %get-tuple-element.28, f32[512]{0:T(512)S(1)} %get-tuple-element.27), channel_id=1, replica_groups=mesh['seq'=16,'wr'=4,'wc'=4] {'wc'}, use_global_device_ids=true, to_apply=%region_11.12 | all-reduce | flops 1024 | bytes 8192 | tf_op jit(solution)/shard_map/psum | solution.py:221
  243.6 6.0 fusion.17
  251.8 32.7 %all_to_all.46 = bf16[512,16,128]{2,0,1:T(8,128)(2,1)S(1)} all-to-all(bf16[512,16,128]{2,0,1:T(8,128)(2,1)S(1)} %bitcast.288), channel_id=1, replica_groups=mesh['seq'=16,'wr'=4,'wc'=4] {'wr','wc'}, dimensions={1} | all-to-all | bytes 4194304 | tf_op jit(solution)/shard_map/all_to_all | solution.py:235
  286.4 46.1 %all-gather.17.cloned.1.call-done = bf16[512,2048]{1,0:T(8,128)(2,1)} async-done(((bf16[512,128]{1,0:T(8,128)(2,1)}), bf16[512,2048]{1,0:T(8,128)(2,1)}) %all-gather.17.cloned.1.call-update) | async-done | bytes 2097168 | tf_op jit(solution)/shard_map/all_gather | solution.py:153
  353.7 8.2 %all-gather.21.cloned.1.call-done = bf16[512,1024]{1,0:T(8,128)(2,1)} async-done(((bf16[512,256]{1,0:T(8,128)(2,1)}), bf16[512,1024]{1,0:T(8,128)(2,1)}) %all-gather.21.cloned.1.call-update) | async-done | bytes 1048592 | tf_op jit(solution)/shard_map/all_gather | solution.py:170
  369.0 17.5 %all-gather.19.cloned.1.call-done = bf16[512,1024]{1,0:T(8,128)(2,1)} async-done(((bf16[512,256]{1,0:T(8,128)(2,1)}), bf16[512,1024]{1,0:T(8,128)(2,1)}) %all-gather.19.cloned.1.call-update) | async-done | bytes 1048592 | tf_op jit(solution)/shard_map/all_gather | solution.py:171
  389.1 3.8 copy.199
  392.9 4.5 fusion.71
  421.6 7.3 %all-to-all-start.3 = ((bf16[16,3,64,256]{3,2,1,0:T(8,128)(2,1)}), bf16[16,3,64,256]{3,2,1,0:T(8,128)(2,1)}, u32[]{:S(2)}, u32[]{:S(2)}) async-start(bf16[16,3,64,256]{3,2,1,0:T(8,128)(2,1)} %pad_maximum_fusion.7), calls=%async_computation.3 | async-start | bytes 3145728 | tf_op jit(solution)/shard_map/all_to_all | solution.py:209
  433.7 58.0 %all-reduce.3 = f32[48]{0:T(128)S(1)} all-reduce(f32[48]{0:T(128)S(1)} %maximum_dynamic-update-slice_fusion.1), channel_id=3, replica_groups=mesh['seq'=16,'wr'=4,'wc'=4] {'seq'}, use_global_device_ids=true, to_apply=%add.3 | all-reduce | flops 48 | bytes 384
  509.2 6.8 %all-to-all-start.4 = ((bf16[16,64,256]{2,1,0:T(8,128)(2,1)}), bf16[16,64,256]{2,1,0:T(8,128)(2,1)}, u32[]{:S(2)}, u32[]{:S(2)}) async-start(bf16[16,64,256]{2,1,0:T(8,128)(2,1)} %multiply_reduce_fusion), calls=%async_computation.4 | async-start | bytes 1048576 | tf_op jit(solution)/shard_map/all_to_all | solution.py:212
  527.5 4.4 all-to-all-done.4
  534.0 7.2 %all-reduce.4 = (f32[512]{0:T(512)S(1)}, f32[512]{0:T(512)S(1)}) all-reduce(f32[512]{0:T(512)S(1)} %get-tuple-element.26, f32[512]{0:T(512)S(1)} %get-tuple-element.25), channel_id=1, replica_groups=mesh['seq'=16,'wr'=4,'wc'=4] {'wc'}, use_global_device_ids=true, to_apply=%region_24.25 | all-reduce | flops 1024 | bytes 8192 | tf_op jit(solution)/shard_map/psum | solution.py:221
  541.3 5.2 fusion.18
  550.0 7.6 %all-to-all-start.5 = ((bf16[512,16,128]{2,0,1:T(8,128)(2,1)}), bf16[512,16,128]{2,0,1:T(8,128)(2,1)S(1)}, u32[]{:S(2)}, u32[]{:S(2)}) async-start(bf16[512,16,128]{2,0,1:T(8,128)(2,1)} %bitcast.287), calls=%async_computation.5 | async-start | bytes 4194304 | tf_op jit(solution)/shard_map/all_to_all | solution.py:235
  559.4 84.2 %psum.39 = bf16[2,3,3,256]{3,1,2,0:T(4,128)(2,1)S(1)} all-reduce(bf16[2,3,3,256]{3,1,2,0:T(4,128)(2,1)S(1)} %copy.221), channel_id=1, replica_groups=mesh['seq'=16,'wr'=4,'wc'=4] {'seq'}, use_global_device_ids=true, to_apply=%region_38.39 | all-reduce | flops 4608 | bytes 18432 | tf_op jit(solution)/shard_map/psum | solution.py:251
  644.5 4.1 copy.271
  (330 shorter events, 182.5 us)
Async XLA Ops:
  7.2 56.5 %all-gather.11.cloned.1.call-start = ((), (), s32[]{:S(2)}) async-start(), calls=%async_computation.6 | async-start | bytes 2228224 | tf_op jit(solution)/shard_map/all_gather | solution.py:153
  7.9 84.7 %all-gather.15.cloned.1.call-start = ((), (), s32[]{:S(2)}) async-start(), calls=%async_computation.8 | async-start | bytes 1310720 | tf_op jit(solution)/shard_map/all_gather | solution.py:170
  12.5 63.7 %copy-start.36 = (s32[512]{0:T(512)}, s32[512]{0:T(512)S(1)}, u32[]{:S(2)}) copy-start(s32[512]{0:T(512)S(1)} %convert_add_fusion) | copy-start | bytes 6148
  69.2 48.1 %all-gather.13.cloned.1.call-start = ((), (), s32[]{:S(2)}) async-start(), calls=%async_computation.7 | async-start | bytes 1310720 | tf_op jit(solution)/shard_map/all_gather | solution.py:171
  72.5 5.3 collective-permute-start
  136.0 71.3 %all-to-all-start = ((bf16[16,3,64,256]{3,2,1,0:T(8,128)(2,1)}), bf16[16,3,64,256]{3,2,1,0:T(8,128)(2,1)}, u32[]{:S(2)}, u32[]{:S(2)}) async-start(bf16[16,3,64,256]{3,2,1,0:T(8,128)(2,1)} %pad_maximum_fusion.6), calls=%async_computation | async-start | bytes 3145728 | tf_op jit(solution)/shard_map/all_to_all | solution.py:209
  146.9 60.4 %copy-start.50 = (s32[17]{0:T(128)}, s32[17]{0:T(128)S(1)}, u32[]{:S(2)}) copy-start(s32[17]{0:T(128)S(1)} %fusion.170) | copy-start | bytes 208
  147.6 59.7 %copy-start.52 = (s32[16]{0:T(128)}, s32[16]{0:T(128)S(1)}, u32[]{:S(2)}) copy-start(s32[16]{0:T(128)S(1)} %fusion.169) | copy-start | bytes 196
  147.6 59.5 %copy-start.31 = (pred[17,16]{0,1:T(8,128)(4,1)}, pred[17,16]{0,1:T(8,128)(4,1)S(1)}, u32[]{:S(2)}) copy-start(pred[17,16]{0,1:T(8,128)(4,1)S(1)} %iota_compare_fusion.2) | copy-start | bytes 820
  147.6 59.5 %copy-start.32 = (pred[16,16]{1,0:T(8,128)(4,1)}, pred[16,16]{1,0:T(8,128)(4,1)S(1)}, u32[]{:S(2)}) copy-start(pred[16,16]{1,0:T(8,128)(4,1)S(1)} %iota_compare_fusion.1) | copy-start | bytes 772
  213.4 20.2 %all-to-all-start.1 = ((bf16[16,64,256]{2,1,0:T(8,128)(2,1)}), bf16[16,64,256]{2,1,0:T(8,128)(2,1)}, u32[]{:S(2)}, u32[]{:S(2)}) async-start(bf16[16,64,256]{2,1,0:T(8,128)(2,1)} %multiply_reduce_fusion.1), calls=%async_computation.1 | async-start | bytes 1048576 | tf_op jit(solution)/shard_map/all_to_all | solution.py:212
  220.2 112.3 %all-gather.17.cloned.1.call-start = ((), (), s32[]{:S(2)}) async-start(), calls=%async_computation.9 | async-start | bytes 2228224 | tf_op jit(solution)/shard_map/all_gather | solution.py:153
  286.1 75.8 %all-gather.21.cloned.1.call-start = ((), (), s32[]{:S(2)}) async-start(), calls=%async_computation.11 | async-start | bytes 1310720 | tf_op jit(solution)/shard_map/all_gather | solution.py:170
  338.5 47.9 %all-gather.19.cloned.1.call-start = ((), (), s32[]{:S(2)}) async-start(), calls=%async_computation.10 | async-start | bytes 1310720 | tf_op jit(solution)/shard_map/all_gather | solution.py:171
  339.2 3.8 collective-permute-start.1
  350.6 38.5 %copy-start.34 = (f32[512]{0:T(512)}, f32[512]{0:T(512)S(1)}, u32[]{:S(2)}) copy-start(f32[512]{0:T(512)S(1)} %get-tuple-element.54) | copy-start | bytes 6148
  421.6 81.6 %all-to-all-start.3 = ((bf16[16,3,64,256]{3,2,1,0:T(8,128)(2,1)}), bf16[16,3,64,256]{3,2,1,0:T(8,128)(2,1)}, u32[]{:S(2)}, u32[]{:S(2)}) async-start(bf16[16,3,64,256]{3,2,1,0:T(8,128)(2,1)} %pad_maximum_fusion.7), calls=%async_computation.3 | async-start | bytes 3145728 | tf_op jit(solution)/shard_map/all_to_all | solution.py:209
  428.9 215.6 %all-gather.23.cloned.1.call-start = ((), (), s32[]{:S(2)}) async-start(), calls=%async_computation.12 | async-start | bytes 1671168 | tf_op jit(solution)/shard_map/all_gather | solution.py:217
  431.7 69.2 %copy-start.51 = (s32[17]{0:T(128)S(1)}, s32[17]{0:T(128)}, u32[]{:S(2)}) copy-start(s32[17]{0:T(128)} %copy-done.50) | copy-start | bytes 208
  431.7 69.2 %copy-start.53 = (s32[16]{0:T(128)S(1)}, s32[16]{0:T(128)}, u32[]{:S(2)}) copy-start(s32[16]{0:T(128)} %copy-done.52) | copy-start | bytes 196
  509.2 22.7 %all-to-all-start.4 = ((bf16[16,64,256]{2,1,0:T(8,128)(2,1)}), bf16[16,64,256]{2,1,0:T(8,128)(2,1)}, u32[]{:S(2)}, u32[]{:S(2)}) async-start(bf16[16,64,256]{2,1,0:T(8,128)(2,1)} %multiply_reduce_fusion), calls=%async_computation.4 | async-start | bytes 1048576 | tf_op jit(solution)/shard_map/all_to_all | solution.py:212
  516.0 134.2 %all-gather.25.cloned.1.call-start = ((), (), s32[]{:S(2)}) async-start(), calls=%async_computation.13 | async-start | bytes 1671168 | tf_op jit(solution)/shard_map/all_gather | solution.py:217
  550.0 93.7 %copy-start.70 = (s32[2]{0:T(128)S(1)}, s32[2]{0:T(128)}, u32[]{:S(2)}) copy-start(s32[2]{0:T(128)} %param.31) | copy-start | bytes 28
  550.0 98.6 %all-to-all-start.5 = ((bf16[512,16,128]{2,0,1:T(8,128)(2,1)}), bf16[512,16,128]{2,0,1:T(8,128)(2,1)S(1)}, u32[]{:S(2)}, u32[]{:S(2)}) async-start(bf16[512,16,128]{2,0,1:T(8,128)(2,1)} %bitcast.287), calls=%async_computation.5 | async-start | bytes 4194304 | tf_op jit(solution)/shard_map/all_to_all | solution.py:235
  (63 other events, 393.7 us)
Sparse Core Ops, SparseCore 0:
  10.6 53.0 all-gather.10
  69.3 23.1 all-gather.14
  94.4 22.8 all-gather.12
  286.2 46.2 all-gather.16
  338.6 23.1 all-gather.20
  363.5 22.8 all-gather.18
  499.2 73.1 all-gather.22
  574.1 70.0 all-gather.24
where the time goes:
time: 669 us; the launch traced here: 664 us
  blocking collectives  246 us (37%)
  waiting for transfers between devices  158 us (24%)
  local copies, waits for them, and re-layouts  72 us (11%)
  other arithmetic  69.9 us (10%)
  matrix products  56.6 us (8%)
  starting transfers between devices  41.7 us (6%)
  between operations  20.6 us (3%)
    unnamed x2, blocking collectives  114 us
    all_gather x2, waiting for transfers between devices, body(): gathered = lax.all_gather(current, ('wr', 'wc'), axis=1, tiled=True)  95.3 us
    psum x1, blocking collectives, body(): edge_stack = lax.psum(jnp.stack(sent_edges), 'seq')  84.2 us
    all_gather x2, waiting for transfers between devices, body(): lax.all_gather(conv_act, 'wc', axis=1, tiled=True)  38.8 us
    all_to_all x1, blocking collectives, body(): lax.all_to_all(term_rows.astype(jnp.bfloat16), ('wr', 'wc'), 1, 0, tiled=...  32.7 us
    unnamed x154, local copies, waits for them, and re-layouts  15 us
    all_to_all x2, starting transfers between devices, body(): got = lax.all_to_all(sent, 'seq', 0, 0, tiled=True).astype(jnp.float32)  14.6 us
    psum x2, blocking collectives, body(): lax.psum((jnp.sum(hidden_parts, axis=1), jnp.sum(hidden_parts * hidden_pa...  14.3 us
  transfers between devices with their start and end apart: 15, of which 9 were waited for; matrix products, arithmetic and copies ran while one was open for 16% of the time, Pallas kernels for 0%

commit v1 on v0

--- a/solution.py
+++ b/solution.py
@@ -11,6 +11,14 @@
 GATE_CAP = 15.0
 ROW_DIMS = (((0,), (0,)), ((), ()))
 FEATURE_DIMS = (((1,), (1,)), ((), ()))
+
+
+def edit_cubes_on_mesh(content, axis_key):
+    u1 = lax.axis_size(axis_key)
+    a_now = jnp.split(content, u1, axis=1)
+    outer = jnp.stack(a_now, axis=0)
+    low = lax.all_to_all(outer, axis_key, 0, 0)
+    return jnp.concatenate(low, axis=0)
 
 
 def shifted(value, axis, steps):
@@ -232,9 +240,9 @@
             * jax.nn.silu(outgate)
         ).astype(jnp.bfloat16)
         term_rows = jnp.dot(gated, w_down[layer_idx], preferred_element_type=jnp.float32)
-        terms = lax.all_to_all(
-            term_rows.astype(jnp.bfloat16), ("wr", "wc"), 1, 0, tiled=True
-        ).reshape(-1, tok_rows, current.shape[1])
+        terms = edit_cubes_on_mesh(term_rows.astype(jnp.bfloat16), ("wr", "wc")).reshape(
+            -1, tok_rows, current.shape[1]
+        )
         summed = jnp.sum(terms.astype(jnp.float32), axis=0)
         current = (current.astype(jnp.float32) + summed).astype(jnp.bfloat16)
         for prompt in range(PROMPTS):

time: 669 us -> 726 us (1.085); the launches traced: 664 us -> 714 us
  local copies, waits for them, and re-layouts: 72 us -> 107 us
  blocking collectives: 246 us -> 263 us
    unnamed x154 -> x168, local copies, waits for them, and re-layouts: 15 us -> 51.5 us
    psum x1, blocking collectives: 84.2 us -> 100 us  [body(): edge_stack = lax.psum(jnp.stack(sent_edges), 'seq')]
  transfers between devices with their start and end apart: 15 -> 15, of which waited for: 9 -> 8; matrix products, arithmetic and copies ran while one was open for 16% -> 19% of each run, Pallas kernels for 0% -> 0%
where the time goes in v1:
time: 726 us; the launch traced here: 714 us
  blocking collectives  263 us (36%)
  waiting for transfers between devices  155 us (21%)
  local copies, waits for them, and re-layouts  107 us (15%)
  other arithmetic  72.6 us (10%)
  matrix products  56.6 us (8%)
  starting transfers between devices  38.8 us (5%)
  between operations  21 us (3%)
    unnamed x2, blocking collectives  115 us
    psum x1, blocking collectives, body(): edge_stack = lax.psum(jnp.stack(sent_edges), 'seq')  100 us
    all_gather x2, waiting for transfers between devices, body(): gathered = lax.all_gather(current, ('wr', 'wc'), axis=1, tiled=True)  96.5 us
    unnamed x168, local copies, waits for them, and re-layouts  51.5 us
    all_gather x2, waiting for transfers between devices, body(): lax.all_gather(conv_act, 'wc', axis=1, tiled=True)  38.8 us
    all_to_all x1, blocking collectives, edit_cubes_on_mesh(): low = lax.all_to_all(outer, axis_key, 0, 0)  32.7 us
    psum x2, blocking collectives, body(): lax.psum((jnp.sum(hidden_parts, axis=1), jnp.sum(hidden_parts * hidden_pa...  15.3 us
    all_to_all x2, starting transfers between devices, body(): got = lax.all_to_all(sent, 'seq', 0, 0, tiled=True).astype(jnp.float32)  14.6 us
  transfers between devices with their start and end apart: 15, of which 8 were waited for; matrix products, arithmetic and copies ran while one was open for 19% of the time, Pallas kernels for 0%

profile of v1, /device:TPU:16, one launch (start us, length us, event | category | flops | bytes accessed | tf_op | source)
XLA Modules:
  0.0 713.7 jit_solution(2202268877119423511)
XLA Ops:
  14.8 48.9 %all-gather.11.cloned.1.call-done = bf16[512,2048]{1,0:T(8,128)(2,1)} async-done(((bf16[512,128]{1,0:T(8,128)(2,1)}), bf16[512,2048]{1,0:T(8,128)(2,1)}) %all-gather.11.cloned.1.call-update) | async-done | bytes 2097168 | tf_op jit(solution)/shard_map/all_gather | solution.py:161
  83.0 3.8 exponential_select_fusion.7
  86.8 5.8 all-gather.15.cloned.1.call-done
  96.0 21.3 %all-gather.13.cloned.1.call-done = bf16[512,1024]{1,0:T(8,128)(2,1)} async-done(((bf16[512,256]{1,0:T(8,128)(2,1)}), bf16[512,1024]{1,0:T(8,128)(2,1)}) %all-gather.13.cloned.1.call-update) | async-done | bytes 1048592 | tf_op jit(solution)/shard_map/all_gather | solution.py:179
  136.1 7.3 %all-to-all-start = ((bf16[16,3,64,256]{3,2,1,0:T(8,128)(2,1)}), bf16[16,3,64,256]{3,2,1,0:T(8,128)(2,1)}, u32[]{:S(2)}, u32[]{:S(2)}) async-start(bf16[16,3,64,256]{3,2,1,0:T(8,128)(2,1)} %pad_maximum_fusion.6), calls=%async_computation | async-start | bytes 3145728 | tf_op jit(solution)/shard_map/all_to_all | solution.py:217
  149.4 56.8 %all-reduce.2 = f32[48]{0:T(128)S(1)} all-reduce(f32[48]{0:T(128)S(1)} %maximum_dynamic-update-slice_fusion), channel_id=2, replica_groups=mesh['seq'=16,'wr'=4,'wc'=4] {'seq'}, use_global_device_ids=true, to_apply=%add.2 | all-reduce | flops 48 | bytes 384
  213.5 6.7 all-to-all-start.1
  236.5 7.7 %all-reduce.5 = (f32[512]{0:T(512)S(1)}, f32[512]{0:T(512)}) all-reduce(f32[512]{0:T(512)S(1)} %get-tuple-element.28, f32[512]{0:T(512)S(1)} %get-tuple-element.27), channel_id=1, replica_groups=mesh['seq'=16,'wr'=4,'wc'=4] {'wc'}, use_global_device_ids=true, to_apply=%region_11.12 | all-reduce | flops 1024 | bytes 8192 | tf_op jit(solution)/shard_map/psum | solution.py:229
  244.9 6.0 convolution_convert_fusion.1
  265.8 32.7 %all_to_all.30 = bf16[16,512,128]{2,1,0:T(8,128)(2,1)S(1)} all-to-all(bf16[16,512,128]{2,1,0:T(8,128)(2,1)S(1)} %fusion.145), channel_id=1, replica_groups=mesh['seq'=16,'wr'=4,'wc'=4] {'wr','wc'}, dimensions={0} | all-to-all | bytes 4194304 | tf_op jit(solution)/shard_map/all_to_all | solution.py:20
  300.4 47.7 %all-gather.17.cloned.1.call-done = bf16[512,2048]{1,0:T(8,128)(2,1)} async-done(((bf16[512,128]{1,0:T(8,128)(2,1)}), bf16[512,2048]{1,0:T(8,128)(2,1)}) %all-gather.17.cloned.1.call-update) | async-done | bytes 2097168 | tf_op jit(solution)/shard_map/all_gather | solution.py:161
  371.1 6.3 all-gather.21.cloned.1.call-done
  384.5 17.5 %all-gather.19.cloned.1.call-done = bf16[512,1024]{1,0:T(8,128)(2,1)} async-done(((bf16[512,256]{1,0:T(8,128)(2,1)}), bf16[512,1024]{1,0:T(8,128)(2,1)}) %all-gather.19.cloned.1.call-update) | async-done | bytes 1048592 | tf_op jit(solution)/shard_map/all_gather | solution.py:179
  404.6 3.8 copy.192
  408.5 4.5 fusion.69
  437.0 7.3 %all-to-all-start.3 = ((bf16[16,3,64,256]{3,2,1,0:T(8,128)(2,1)}), bf16[16,3,64,256]{3,2,1,0:T(8,128)(2,1)}, u32[]{:S(2)}, u32[]{:S(2)}) async-start(bf16[16,3,64,256]{3,2,1,0:T(8,128)(2,1)} %pad_maximum_fusion.7), calls=%async_computation.3 | async-start | bytes 3145728 | tf_op jit(solution)/shard_map/all_to_all | solution.py:217
  449.4 57.7 %all-reduce.3 = f32[48]{0:T(128)S(1)} all-reduce(f32[48]{0:T(128)S(1)} %maximum_dynamic-update-slice_fusion.1), channel_id=3, replica_groups=mesh['seq'=16,'wr'=4,'wc'=4] {'seq'}, use_global_device_ids=true, to_apply=%add.3 | all-reduce | flops 48 | bytes 384
  523.7 6.7 all-to-all-start.4
  542.0 5.0 all-to-all-done.4
  549.2 7.6 %all-reduce.4 = (f32[512]{0:T(512)S(1)}, f32[512]{0:T(512)S(1)}) all-reduce(f32[512]{0:T(512)S(1)} %get-tuple-element.26, f32[512]{0:T(512)S(1)} %get-tuple-element.25), channel_id=1, replica_groups=mesh['seq'=16,'wr'=4,'wc'=4] {'wc'}, use_global_device_ids=true, to_apply=%region_24.25 | all-reduce | flops 1024 | bytes 8192 | tf_op jit(solution)/shard_map/psum | solution.py:229
  556.8 5.2 convolution_convert_fusion
  587.0 5.2 all-to-all-start.5
  592.7 100.3 %psum.39 = bf16[2,3,3,256]{3,1,2,0:T(4,128)(2,1)S(1)} all-reduce(bf16[2,3,3,256]{3,1,2,0:T(4,128)(2,1)S(1)} %copy.213), channel_id=1, replica_groups=mesh['seq'=16,'wr'=4,'wc'=4] {'seq'}, use_global_device_ids=true, to_apply=%region_38.39 | all-reduce | flops 4608 | bytes 18432 | tf_op jit(solution)/shard_map/psum | solution.py:259
  693.9 4.1 copy.257
  (344 shorter events, 216.6 us)
Async XLA Ops:
  7.2 56.5 %all-gather.11.cloned.1.call-start = ((), (), s32[]{:S(2)}) async-start(), calls=%async_computation.6 | async-start | bytes 2228224 | tf_op jit(solution)/shard_map/all_gather | solution.py:161
  7.9 84.7 %all-gather.15.cloned.1.call-start = ((), (), s32[]{:S(2)}) async-start(), calls=%async_computation.8 | async-start | bytes 1310720 | tf_op jit(solution)/shard_map/all_gather | solution.py:178
  12.7 63.1 %copy-start.32 = (s32[512]{0:T(512)}, s32[512]{0:T(512)S(1)}, u32[]{:S(2)}) copy-start(s32[512]{0:T(512)S(1)} %convert_add_fusion) | copy-start | bytes 6148
  69.3 48.1 %all-gather.13.cloned.1.call-start = ((), (), s32[]{:S(2)}) async-start(), calls=%async_computation.7 | async-start | bytes 1310720 | tf_op jit(solution)/shard_map/all_gather | solution.py:179
  72.6 4.8 collective-permute-start
  136.1 71.3 %all-to-all-start = ((bf16[16,3,64,256]{3,2,1,0:T(8,128)(2,1)}), bf16[16,3,64,256]{3,2,1,0:T(8,128)(2,1)}, u32[]{:S(2)}, u32[]{:S(2)}) async-start(bf16[16,3,64,256]{3,2,1,0:T(8,128)(2,1)} %pad_maximum_fusion.6), calls=%async_computation | async-start | bytes 3145728 | tf_op jit(solution)/shard_map/all_to_all | solution.py:217
  146.5 60.8 %copy-start.47 = (s32[17]{0:T(128)}, s32[17]{0:T(128)S(1)}, u32[]{:S(2)}) copy-start(s32[17]{0:T(128)S(1)} %fusion.200) | copy-start | bytes 208
  147.3 60.1 %copy-start.48 = (s32[16]{0:T(128)}, s32[16]{0:T(128)S(1)}, u32[]{:S(2)}) copy-start(s32[16]{0:T(128)S(1)} %fusion.199) | copy-start | bytes 196
  147.3 59.8 %copy-start.27 = (pred[17,16]{0,1:T(8,128)(4,1)}, pred[17,16]{0,1:T(8,128)(4,1)S(1)}, u32[]{:S(2)}) copy-start(pred[17,16]{0,1:T(8,128)(4,1)S(1)} %iota_compare_fusion.2) | copy-start | bytes 820
  147.3 59.8 %copy-start.28 = (pred[16,16]{1,0:T(8,128)(4,1)}, pred[16,16]{1,0:T(8,128)(4,1)S(1)}, u32[]{:S(2)}) copy-start(pred[16,16]{1,0:T(8,128)(4,1)S(1)} %iota_compare_fusion.1) | copy-start | bytes 772
  213.5 20.2 %all-to-all-start.1 = ((bf16[16,64,256]{2,1,0:T(8,128)(2,1)}), bf16[16,64,256]{2,1,0:T(8,128)(2,1)}, u32[]{:S(2)}, u32[]{:S(2)}) async-start(bf16[16,64,256]{2,1,0:T(8,128)(2,1)} %multiply_reduce_fusion.1), calls=%async_computation.1 | async-start | bytes 1048576 | tf_op jit(solution)/shard_map/all_to_all | solution.py:220
  220.2 127.8 %all-gather.17.cloned.1.call-start = ((), (), s32[]{:S(2)}) async-start(), calls=%async_computation.9 | async-start | bytes 2228224 | tf_op jit(solution)/shard_map/all_gather | solution.py:161
  300.1 77.3 %all-gather.21.cloned.1.call-start = ((), (), s32[]{:S(2)}) async-start(), calls=%async_computation.11 | async-start | bytes 1310720 | tf_op jit(solution)/shard_map/all_gather | solution.py:178
  354.1 47.9 %all-gather.19.cloned.1.call-start = ((), (), s32[]{:S(2)}) async-start(), calls=%async_computation.10 | async-start | bytes 1310720 | tf_op jit(solution)/shard_map/all_gather | solution.py:179
  356.2 5.3 collective-permute-start.1
  368.0 36.6 %copy-start.30 = (f32[512]{0:T(512)}, f32[512]{0:T(512)S(1)}, u32[]{:S(2)}) copy-start(f32[512]{0:T(512)S(1)} %get-tuple-element.54) | copy-start | bytes 6148
  437.0 80.6 %all-to-all-start.3 = ((bf16[16,3,64,256]{3,2,1,0:T(8,128)(2,1)}), bf16[16,3,64,256]{3,2,1,0:T(8,128)(2,1)}, u32[]{:S(2)}, u32[]{:S(2)}) async-start(bf16[16,3,64,256]{3,2,1,0:T(8,128)(2,1)} %pad_maximum_fusion.7), calls=%async_computation.3 | async-start | bytes 3145728 | tf_op jit(solution)/shard_map/all_to_all | solution.py:217
  444.3 249.5 %all-gather.23.cloned.1.call-start = ((), (), s32[]{:S(2)}) async-start(), calls=%async_computation.12 | async-start | bytes 1671168 | tf_op jit(solution)/shard_map/all_gather | solution.py:225
  523.7 23.3 %all-to-all-start.4 = ((bf16[16,64,256]{2,1,0:T(8,128)(2,1)}), bf16[16,64,256]{2,1,0:T(8,128)(2,1)}, u32[]{:S(2)}, u32[]{:S(2)}) async-start(bf16[16,64,256]{2,1,0:T(8,128)(2,1)} %multiply_reduce_fusion), calls=%async_computation.4 | async-start | bytes 1048576 | tf_op jit(solution)/shard_map/all_to_all | solution.py:220
  530.5 167.5 %all-gather.25.cloned.1.call-start = ((), (), s32[]{:S(2)}) async-start(), calls=%async_computation.13 | async-start | bytes 1671168 | tf_op jit(solution)/shard_map/all_gather | solution.py:225
  541.2 15.5 %copy-start.4 = (bf16[512,2048]{1,0:T(8,128)(2,1)S(1)}, bf16[512,2048]{1,0:T(8,128)(2,1)}, u32[]{:S(2)}) copy-start(bf16[512,2048]{1,0:T(8,128)(2,1)} %copy-done.3) | copy-start | bytes 6291460
  541.3 15.5 %copy-start.19 = (bf16[512,256]{1,0:T(8,128)(2,1)S(1)}, bf16[512,256]{1,0:T(8,128)(2,1)}, u32[]{:S(2)}) copy-start(bf16[512,256]{1,0:T(8,128)(2,1)} %multiply_convert_fusion.3) | copy-start | bytes 786436
  587.0 106.0 %copy-start.62 = (s32[2]{0:T(128)S(1)}, s32[2]{0:T(128)}, u32[]{:S(2)}) copy-start(s32[2]{0:T(128)} %param.31) | copy-start | bytes 28
  587.0 118.1 %all-to-all-start.5 = ((bf16[16,512,128]{2,1,0:T(8,128)(2,1)}), bf16[16,512,128]{2,1,0:T(8,128)(2,1)S(1)}, u32[]{:S(2)}, u32[]{:S(2)}) async-start(bf16[16,512,128]{2,1,0:T(8,128)(2,1)} %fusion.129), calls=%async_computation.5 | async-start | bytes 4194304 | tf_op jit(solution)/shard_map/all_to_all | solution.py:20
  (55 other events, 294.7 us)
Sparse Core Ops, SparseCore 0:
  10.6 53.0 all-gather.10
  69.4 23.1 all-gather.14
  94.4 22.8 all-gather.12
  300.3 47.7 all-gather.16
  354.2 23.1 all-gather.20
  379.1 22.8 all-gather.18
  514.8 72.4 all-gather.22
  589.1 70.6 all-gather.24
